TPU v7x, 128 devices: a whole 4x4x4 slice. The times are simulated.
128 devices in a mesh: blk: 16 (over y, z), rep: 8 (over x, core).
Axes of the slice: x: 4, y: 4, z: 4, core: 2. Of those that a mesh axis runs over, the one named last changes fastest.
Arguments:
- dense: bfloat16 [131072, 1024], P(('blk', 'rep')), may hold values from -6 to 6
- labels: int32 [131072], P(('blk', 'rep')), may hold values 0 or 1
- tile_values: bfloat16 [16384, 64, 128], P(('blk', 'rep')), may hold values from -1.1953125 to 1.1953125
- tile_block: int32 [16384, 64], P(('blk', 'rep')), may hold values from 0 to 1023
- tile_example: int32 [16384, 64], P(('blk', 'rep')), may hold values from 0 to 1023
- tile_count: int32 [16384], P(('blk', 'rep')), may hold values from 16 to 64, as said below
- z_state: float32 [131072, 128], P(('blk', 'rep')), may hold values from -6 to 6
- n_state: float32 [131072, 128], P(('blk', 'rep')), may hold values from 0.01 to 4
- w_one: bfloat16 [1024, 512], replicated, may hold values from -0.1875 to 0.1875
- b_one: float32 [512], replicated, may hold values from -3 to 3
- w_two: bfloat16 [512, 256], replicated, may hold values from -0.25 to 0.25
- b_two: float32 [256], replicated, may hold values from -3 to 3
- head: bfloat16 [256], replicated, may hold values from -0.375 to 0.375
Outputs:
- probability: float32 [131072], P(('blk', 'rep'))
- z_new: float32 [131072, 128], P(('blk', 'rep'))
- n_new: float32 [131072, 128], P(('blk', 'rep'))
- grad_w_one: float32 [1024, 512], replicated
- grad_b_one: float32 [512], replicated
- grad_w_two: float32 [512, 256], replicated
- grad_b_two: float32 [256], replicated
- grad_head: float32 [256], replicated
Inputs may be any that keep to these rules, and one draw needn't show every extreme that they name: `tile_count`: slots at or beyond a list's count are padding; in every draw some owners receive 64 live slots from every device.
All inputs are finite; a program needn't handle non-finite values. No bound on the sum of `labels` on one device may be relied on, other than what follows from the above.
Results may differ from a plain program's by a relative error of at most 0.013.
Values may be sent and summed in bfloat16 or wider, within the bound.
A program may use at most 64 MiB of HBM per device.

v0:
```python
import jax
import jax.numpy as jnp
from jax import lax
from jax.sharding import PartitionSpec as P

alpha_rate = 0.5
beta_shift = 1.0
lasso_term = 0.5
ridge_term = 0.1


def wide_weight(z_state, n_state):
    shrunk = z_state - jnp.sign(z_state) * lasso_term
    denominator = (beta_shift + jnp.sqrt(n_state)) / alpha_rate + ridge_term
    return jnp.where(jnp.abs(z_state) > lasso_term, -shrunk / denominator, jnp.zeros_like(z_state))


def silu_slope(pre):
    gate = jax.nn.sigmoid(pre)
    return gate * (1.0 + pre * (1.0 - gate))


def per_device(
    dense,
    labels,
    tile_values,
    tile_block,
    tile_example,
    tile_count,
    z_state,
    n_state,
    w_one,
    b_one,
    w_two,
    b_two,
    head,
):
    owners, capacity, width = tile_values.shape
    slots = jnp.arange(capacity, dtype=jnp.int32)
    live = slots[None, :] < tile_count[:, None]
    masked = jnp.where(live[:, :, None], tile_values, jnp.zeros_like(tile_values))
    got_values, got_block = (
        lax.all_to_all(masked, ("blk", "rep"), split_axis=0, concat_axis=0, tiled=True),
        lax.all_to_all(tile_block, ("blk", "rep"), split_axis=0, concat_axis=0, tiled=True),
    )
    weight = wide_weight(z_state, n_state)
    flat_block = got_block.reshape(-1)
    flat_values = got_values.reshape(-1, width)
    picked = jnp.take(weight, flat_block, axis=0)
    tile_logit = jnp.sum(flat_values.astype(jnp.float32) * picked, axis=1).reshape(owners, capacity)
    returned = lax.all_to_all(tile_logit, ("blk", "rep"), split_axis=0, concat_axis=0, tiled=True)
    flat_example = tile_example.reshape(-1)
    wide = jnp.zeros((dense.shape[0],), jnp.float32).at[flat_example].add(returned.reshape(-1))
    pre_one = jnp.dot(dense, w_one, preferred_element_type=jnp.float32) + b_one
    hid_one = jax.nn.silu(pre_one).astype(jnp.bfloat16)
    pre_two = jnp.dot(hid_one, w_two, preferred_element_type=jnp.float32) + b_two
    hid_two = jax.nn.silu(pre_two).astype(jnp.bfloat16)
    deep = jnp.dot(hid_two, head, preferred_element_type=jnp.float32)
    probability = jax.nn.sigmoid(wide + deep)
    residual = probability - labels.astype(jnp.float32)
    tile_residual = jnp.take(residual, flat_example).reshape(owners, capacity)
    got_residual = lax.all_to_all(
        tile_residual, ("blk", "rep"), split_axis=0, concat_axis=0, tiled=True
    )
    contrib = flat_values.astype(jnp.float32) * got_residual.reshape(-1)[:, None]
    grad_block = jnp.zeros_like(z_state).at[flat_block].add(contrib)
    n_new = n_state + grad_block * grad_block
    sigma = (jnp.sqrt(n_new) - jnp.sqrt(n_state)) / alpha_rate
    z_new = z_state + grad_block - sigma * weight
    dlogit = residual.astype(jnp.bfloat16)
    grad_head = jnp.dot(dlogit, hid_two, preferred_element_type=jnp.float32)
    d_two = (
        dlogit.astype(jnp.float32)[:, None]
        * head.astype(jnp.float32)[None, :]
        * silu_slope(pre_two)
    ).astype(jnp.bfloat16)
    grad_w_two = lax.dot_general(
        hid_one, d_two, (((0,), (0,)), ((), ())), preferred_element_type=jnp.float32
    )
    grad_b_two = jnp.sum(d_two.astype(jnp.float32), axis=0)
    back_one = lax.dot_general(
        d_two, w_two, (((1,), (1,)), ((), ())), preferred_element_type=jnp.float32
    )
    d_one = (back_one * silu_slope(pre_one)).astype(jnp.bfloat16)
    grad_w_one = lax.dot_general(
        dense, d_one, (((0,), (0,)), ((), ())), preferred_element_type=jnp.float32
    )
    grad_b_one = jnp.sum(d_one.astype(jnp.float32), axis=0)
    grad_head, grad_w_two, grad_b_two, grad_w_one, grad_b_one = lax.psum(
        (grad_head, grad_w_two, grad_b_two, grad_w_one, grad_b_one), ("blk", "rep")
    )
    return (probability, z_new, n_new, grad_w_one, grad_b_one, grad_w_two, grad_b_two, grad_head)


def solution(mesh):
    placed = (
        P(("blk", "rep"), None),
        P(("blk", "rep")),
        P(("blk", "rep"), None, None),
        P(("blk", "rep"), None),
        P(("blk", "rep"), None),
        P(("blk", "rep")),
        P(("blk", "rep"), None),
        P(("blk", "rep"), None),
        P(),
        P(),
        P(),
        P(),
        P(),
    )
    return jax.shard_map(
        per_device,
        mesh=mesh,
        in_specs=placed,
        out_specs=(
            P(("blk", "rep")),
            P(("blk", "rep"), None),
            P(("blk", "rep"), None),
            P(),
            P(),
            P(),
            P(),
            P(),
        ),
        check_vma=False,
    )
```

profile of v0, /device:TPU:1, one launch (start us, length us, event | category | flops | bytes accessed | tf_op | source)
XLA Modules:
  0.0 373.5 jit_solution(6273867925865264041)
XLA Ops:
  7.2 0.0 copy-start
  7.2 1.6 copy.30
  8.8 11.5 %all-to-all-start.1 = ((s32[128,1,64]{2,1,0:T(1,128)}), s32[128,1,64]{2,1,0:T(1,128)S(1)}, u32[]{:S(2)}, u32[]{:S(2)}) async-start(s32[128,1,64]{2,1,0:T(1,128)} %bitcast.2), calls=%async_computation.1 | async-start | bytes 131072 | tf_op jit(solution)/shard_map/all_to_all | solution.py:44
  20.3 0.7 iota_compare_fusion
  21.1 0.7 reshape.183
  21.7 0.8 copy.29
  22.6 0.1 reshape.146
  22.7 1.6 divide_select_fusion
  24.4 0.0 copy-start.5
  24.4 0.0 copy-start.8
  24.4 4.5 %broadcast_select_fusion = bf16[128,64,128]{2,1,0:T(8,128)(2,1)} fusion(bf16[128,64,128]{2,1,0:T(8,128)(2,1)} %param.15, pred[128,64]{1,0:T(8,128)(4,1)S(1)} %iota_compare_fusion), kind=kLoop, calls=%fused_computation.10 | loop fusion | flops 1048576 | bytes 4202496 | tf_op jit(solution)/shard_map/jit(_where)/select_n | solution.py:41
  29.0 2.8 multiply_convert_fusion.1
  31.7 1.4 multiply_convert_fusion.3
  33.1 0.2 fusion.3
  33.4 10.2 %all-to-all-start = ((bf16[128,64,128]{2,1,0:T(8,128)(2,1)}), bf16[128,64,128]{2,1,0:T(8,128)(2,1)}, u32[]{:S(2)}, u32[]{:S(2)}) async-start(bf16[128,64,128]{2,1,0:T(8,128)(2,1)} %broadcast_select_fusion), calls=%async_computation | async-start | bytes 4194304 | tf_op jit(solution)/shard_map/all_to_all | solution.py:43
  43.6 0.5 broadcast.153
  44.1 0.8 reduce.10
  44.9 0.1 reshape.148
  45.1 27.8 %gather_fusion = f32[8192,128]{1,0:T(8,128)} fusion(f32[1024,128]{1,0:T(8,128)S(1)} %divide_select_fusion, s32[8192]{0:T(1024)S(1)} %broadcast_clamp_fusion.1), kind=kCustom, calls=%fused_computation | custom fusion | bytes 8421376 | tf_op jit(solution)/shard_map/jit(_take)/gather | solution.py:49
  72.9 0.9 all-to-all-done
  73.8 5.4 %multiply_reduce_fusion = f32[128,64]{1,0:T(8,128)} fusion(f32[128,64,128]{2,1,0:T(8,128)} %bitcast.30, pred[128,64]{1,0:T(8,128)(4,1)S(1)} %compare_and_fusion, bf16[128,64,128]{2,1,0:T(8,128)(2,1)} %all-to-all-done), kind=kLoop, calls=%fused_computation.5 | loop fusion | flops 4186112 | bytes 6332416 | tf_op jit(solution)/shard_map/reduce_sum | solution.py:50
  79.2 8.9 %all-to-all-start.2 = ((f32[128,1,64]{2,1,0:T(1,128)}), f32[128,1,64]{2,1,0:T(1,128)S(1)}, u32[]{:S(2)}, u32[]{:S(2)}) async-start(f32[128,1,64]{2,1,0:T(1,128)} %bitcast.6), calls=%async_computation.2 | async-start | bytes 131072 | tf_op jit(solution)/shard_map/all_to_all | solution.py:51
  88.2 9.4 %all-to-all-done.2 = f32[128,1,64]{2,1,0:T(1,128)S(1)} async-done(((f32[128,1,64]{2,1,0:T(1,128)}), f32[128,1,64]{2,1,0:T(1,128)S(1)}, u32[]{:S(2)}, u32[]{:S(2)}) %all-to-all-start.2) | async-done | bytes 32800 | tf_op jit(solution)/shard_map/all_to_all | solution.py:51
  97.5 0.5 broadcast.154
  98.0 0.8 reduce.11
  98.9 0.1 reshape.171
  98.9 57.0 %scatter_fusion = f32[1024]{0:T(1024)S(1)} fusion(f32[1024]{0:T(1024)S(1)} %bitcast.29, s32[8192]{0:T(1024)S(1)} %bitcast.33, f32[8192]{0:T(1024)S(1)} %reshape.171), kind=kCustom, calls=%fused_computation.2 | custom fusion | flops 8192 | bytes 131072 | tf_op jit(solution)/shard_map/scatter-add | solution.py:53
  156.0 0.6 fusion.2
  156.6 1.8 convert_reduce_fusion.1
  158.3 2.5 fusion.4
  160.8 1.0 convert_reduce_fusion
  161.9 2.6 convolution_bitcast_fusion
  164.5 32.9 %gather_fusion.1 = f32[8192]{0:T(1024)S(1)} fusion(f32[1024]{0:T(1024)S(1)} %get-tuple-element.41, s32[8192]{0:T(1024)S(1)} %broadcast_clamp_fusion), kind=kCustom, calls=%fused_computation.1 | custom fusion | bytes 98304 | tf_op jit(solution)/shard_map/jit(_take)/gather | solution.py:61
  197.4 0.1 gather.15
  197.4 0.7 and_select_fusion
  198.1 4.6 %all-to-all-start.3 = ((f32[128,1,64]{2,1,0:T(1,128)}), f32[128,1,64]{2,1,0:T(1,128)S(1)}, u32[]{:S(2)}, u32[]{:S(2)}) async-start(f32[128,1,64]{2,1,0:T(1,128)} %bitcast.9), calls=%async_computation.3 | async-start | bytes 131072 | tf_op jit(solution)/shard_map/all_to_all | solution.py:62
  202.7 0.0 all-reduce.4.cloned.1.call-start
  202.8 0.2 fusion.5
  202.9 0.5 all-reduce.4.cloned.1.call-update
  203.4 67.4 %all-reduce = (f32[512]{0:T(512)}, f32[256]{0:T(256)}, f32[256]{0:T(256)}) all-reduce(f32[512]{0:T(512)S(1)} %get-tuple-element.49, f32[256]{0:T(256)S(1)} %get-tuple-element.37, f32[256]{0:T(256)S(1)} %bitcast.36), channel_id=1, replica_groups=mesh['blk'=16,'rep'=8] {'blk','rep'}, use_global_device_ids=true, to_apply=%region_5.6 | all-reduce | flops 1024 | bytes 8192 | tf_op jit(solution)/shard_map/psum | solution.py:89
  270.9 0.8 reduce.12
  271.7 0.1 mul.66
  271.8 3.9 %bitcast_multiply_fusion = f32[8192,128]{1,0:T(8,128)} fusion(f32[8192]{0:T(1024)S(1)} %mul.66, bf16[128,64,128]{2,1,0:T(8,128)(2,1)} %all-to-all-done), kind=kLoop, calls=%fused_computation.4 | loop fusion | flops 2097152 | bytes 6324224 | tf_op jit(solution)/shard_map/mul | solution.py:65
  275.7 45.1 %scatter_custom_fusion.1 = f32[1024,128]{1,0:T(8,128)} fusion(s32[8192]{0:T(1024)S(1)} %bitcast.35, f32[8192,128]{1,0:T(8,128)} %bitcast_multiply_fusion, f32[]{:T(128)} %constant.32.clone.1), kind=kCustom, calls=%fused_computation.21 | custom fusion | flops 1048576 | bytes 524800 | tf_op jit(solution)/shard_map/scatter-add | solution.py:66
  320.7 2.7 multiply_subtract_fusion
  323.4 39.5 %all-reduce.4.cloned.1.call-done = (f32[1024,512]{0,1:T(8,128)}, f32[512,256]{1,0:T(8,128)}) async-done(((f32[1024,512]{0,1:T(8,128)}, f32[512,256]{1,0:T(8,128)}), (f32[1024,512]{0,1:T(8,128)}, f32[512,256]{1,0:T(8,128)})) %all-reduce.4.cloned.1.call-update) | async-done | bytes 2621456 | tf_op jit(solution)/shard_map/psum | solution.py:89
  362.9 2.9 copy.35
  365.8 0.8 copy.39
  (32 shorter events, 0.2 us)
Async XLA Ops:
  7.2 21.8 %copy-start = (bf16[1024,1024]{1,0:T(8,128)(2,1)S(1)}, bf16[1024,1024]{1,0:T(8,128)(2,1)}, u32[]{:S(2)}) copy-start(bf16[1024,1024]{1,0:T(8,128)(2,1)} %param.13) | copy-start | bytes 6291460
  8.8 24.6 %all-to-all-start.1 = ((s32[128,1,64]{2,1,0:T(1,128)}), s32[128,1,64]{2,1,0:T(1,128)S(1)}, u32[]{:S(2)}, u32[]{:S(2)}) async-start(s32[128,1,64]{2,1,0:T(1,128)} %bitcast.2), calls=%async_computation.1 | async-start | bytes 131072 | tf_op jit(solution)/shard_map/all_to_all | solution.py:44
  24.4 4.6 %copy-start.5 = (bf16[1024,512]{1,0:T(8,128)(2,1)S(1)}, bf16[1024,512]{1,0:T(8,128)(2,1)}, u32[]{:S(2)}) copy-start(bf16[1024,512]{1,0:T(8,128)(2,1)} %param.21) | copy-start | bytes 3145732
  24.4 4.5 %copy-start.8 = (f32[512]{0:T(512)S(1)}, f32[512]{0:T(512)}, u32[]{:S(2)}) copy-start(f32[512]{0:T(512)} %param.22) | copy-start | bytes 6148
  28.9 2.8 copy-start.6
  28.9 2.8 copy-start.9
  31.7 1.4 copy-start.11
  33.4 40.4 %all-to-all-start = ((bf16[128,64,128]{2,1,0:T(8,128)(2,1)}), bf16[128,64,128]{2,1,0:T(8,128)(2,1)}, u32[]{:S(2)}, u32[]{:S(2)}) async-start(bf16[128,64,128]{2,1,0:T(8,128)(2,1)} %broadcast_select_fusion), calls=%async_computation | async-start | bytes 4194304 | tf_op jit(solution)/shard_map/all_to_all | solution.py:43
  73.8 14.3 %copy-start.10 = (bf16[256]{0:T(256)(128)(2,1)S(1)}, bf16[256]{0:T(256)(128)(2,1)}, u32[]{:S(2)}) copy-start(bf16[256]{0:T(256)(128)(2,1)} %param.25) | copy-start | bytes 1540
  79.2 18.3 %all-to-all-start.2 = ((f32[128,1,64]{2,1,0:T(1,128)}), f32[128,1,64]{2,1,0:T(1,128)S(1)}, u32[]{:S(2)}, u32[]{:S(2)}) async-start(f32[128,1,64]{2,1,0:T(1,128)} %bitcast.6), calls=%async_computation.2 | async-start | bytes 131072 | tf_op jit(solution)/shard_map/all_to_all | solution.py:51
  98.9 57.0 %copy-start.4 = (s32[1024]{0:T(1024)S(1)}, s32[1024]{0:T(1024)}, u32[]{:S(2)}) copy-start(s32[1024]{0:T(1024)} %param.14) | copy-start | bytes 12292
  156.0 4.9 %copy-start.7 = (bf16[512,256]{1,0:T(8,128)(2,1)S(1)}, bf16[512,256]{1,0:T(8,128)(2,1)}, u32[]{:S(2)}) copy-start(bf16[512,256]{1,0:T(8,128)(2,1)} %param.23) | copy-start | bytes 786436
  156.0 4.9 %copy-start.12 = (f32[1024,512]{1,0:T(8,128)S(1)}, f32[1024,512]{1,0:T(8,128)}, u32[]{:S(2)}) copy-start(f32[1024,512]{1,0:T(8,128)} %get-tuple-element.46) | copy-start | bytes 6291460
  198.1 72.8 %all-to-all-start.3 = ((f32[128,1,64]{2,1,0:T(1,128)}), f32[128,1,64]{2,1,0:T(1,128)S(1)}, u32[]{:S(2)}, u32[]{:S(2)}) async-start(f32[128,1,64]{2,1,0:T(1,128)} %bitcast.9), calls=%async_computation.3 | async-start | bytes 131072 | tf_op jit(solution)/shard_map/all_to_all | solution.py:62
  202.7 160.2 %all-reduce.4.cloned.1.call-start = ((), (), s32[]{:S(2)}) async-start(), calls=%async_computation.4 | async-start | bytes 5242880 | tf_op jit(solution)/shard_map/psum | solution.py:89
  271.8 49.0 %copy-start.1 = (f32[1024,128]{1,0:T(8,128)S(1)}, f32[1024,128]{1,0:T(8,128)}, u32[]{:S(2)}) copy-start(f32[1024,128]{1,0:T(8,128)} %param.19) | copy-start | bytes 1572868
  271.8 49.0 %copy-start.2 = (f32[1024,128]{1,0:T(8,128)S(1)}, f32[1024,128]{1,0:T(8,128)}, u32[]{:S(2)}) copy-start(f32[1024,128]{1,0:T(8,128)} %param.20) | copy-start | bytes 1572868
  362.9 2.9 copy-start.3
Sparse Core Ops, SparseCore 0:
  209.1 153.7 all-reduce.3
where the time goes:
time: 374 us; the launch traced here: 373 us
  other arithmetic  127 us (34%)
  local copies, waits for them, and re-layouts  69 us (18%)
  blocking collectives  67.4 us (18%)
  waiting for transfers between devices  50.3 us (13%)
  starting transfers between devices  35.3 us (9%)
  between operations  14.3 us (4%)
  matrix products  10.7 us (3%)
    psum x1, blocking collectives, per_device(): lax.psum((grad_head, grad_w_two, grad_b_two, grad_w_one, grad_b_one), ('b...  67.4 us
    scatter-add x1, other arithmetic, per_device(): jnp.zeros((dense.shape[0],), jnp.float32).at[flat_example]  57 us
    scatter-add x1, other arithmetic, per_device(): grad_block = jnp.zeros_like(z_state).at[flat_block].add(contrib)  45.1 us
    psum x1, waiting for transfers between devices, per_device(): lax.psum((grad_head, grad_w_two, grad_b_two, grad_w_one, grad_b_one), ('b...  39.5 us
    gather x2, local copies, waits for them, and re-layouts, per_device(): tile_residual = jnp.take(residual, flat_example).reshape(owners, capacity)  32.9 us
    gather x1, local copies, waits for them, and re-layouts, per_device(): picked = jnp.take(weight, flat_block, axis=0)  27.8 us
    all_to_all x1, starting transfers between devices, per_device(): lax.all_to_all(tile_block, ('blk', 'rep'), split_axis=0, concat_axis=0, t...  11.5 us
    all_to_all x1, starting transfers between devices, per_device(): lax.all_to_all(masked, ('blk', 'rep'), split_axis=0, concat_axis=0, tiled...  10.2 us
  transfers between devices with their start and end apart: 5, of which 3 were waited for; matrix products, arithmetic and copies ran while one was open for 25% of the time, Pallas kernels for 0%

commit v1 on v0

--- a/solution.py
+++ b/solution.py
@@ -2,6 +2,7 @@
 import jax.numpy as jnp
 from jax import lax
 from jax.sharding import PartitionSpec as P
+from jax.lax import psum
 
 alpha_rate = 0.5
 beta_shift = 1.0
@@ -86,8 +87,8 @@
         dense, d_one, (((0,), (0,)), ((), ())), preferred_element_type=jnp.float32
     )
     grad_b_one = jnp.sum(d_one.astype(jnp.float32), axis=0)
-    grad_head, grad_w_two, grad_b_two, grad_w_one, grad_b_one = lax.psum(
-        (grad_head, grad_w_two, grad_b_two, grad_w_one, grad_b_one), ("blk", "rep")
+    grad_head, grad_w_two, grad_b_two, grad_w_one, grad_b_one = psum(
+        psum((grad_head, grad_w_two, grad_b_two, grad_w_one, grad_b_one), "rep"), "blk"
     )
     return (probability, z_new, n_new, grad_w_one, grad_b_one, grad_w_two, grad_b_two, grad_head)
 

time: 374 us -> 356 us (0.952)
  the two profiles are of different devices: /device:TPU:1 before, /device:TPU:0 now
where the time goes in v1:
time: 356 us
  other arithmetic  125 us (35%)
  local copies, waits for them, and re-layouts  68.7 us (19%)
  blocking collectives  57.1 us (16%)
  waiting for transfers between devices  40.4 us (11%)
  starting transfers between devices  39 us (11%)
  between operations  14.3 us (4%)
  matrix products  10.9 us (3%)
    scatter-add x1, other arithmetic, per_device(): jnp.zeros((dense.shape[0],), jnp.float32).at[flat_example]  57 us
    scatter-add x1, other arithmetic, per_device(): grad_block = jnp.zeros_like(z_state).at[flat_block].add(contrib)  45.1 us
    psum x1, blocking collectives, per_device(): psum(psum((grad_head, grad_w_two, grad_b_two, grad_w_one, grad_b_one), 'r...  42.1 us
    gather x2, local copies, waits for them, and re-layouts, per_device(): tile_residual = jnp.take(residual, flat_example).reshape(owners, capacity)  33 us
    psum x1, waiting for transfers between devices, per_device(): psum((grad_head, grad_w_two, grad_b_two, grad_w_one, grad_b_one), 'rep')  30.7 us
    gather x1, local copies, waits for them, and re-layouts, per_device(): picked = jnp.take(weight, flat_block, axis=0)  27.8 us
    psum x1, blocking collectives, per_device(): psum((grad_head, grad_w_two, grad_b_two, grad_w_one, grad_b_one), 'rep')  15 us
    all_to_all x1, starting transfers between devices, per_device(): lax.all_to_all(tile_block, ('blk', 'rep'), split_axis=0, concat_axis=0, t...  11.1 us
  transfers between devices with their start and end apart: 6, of which 3 were waited for; matrix products, arithmetic and copies ran while one was open for 36% of the time, Pallas kernels for 0%

profile of v1, /device:TPU:0, one launch (start us, length us, event | category | flops | bytes accessed | tf_op | source)
XLA Modules:
  0.0 355.6 jit_solution(14354165071060389675)
XLA Ops:
  7.2 1.6 copy.30
  8.8 11.1 %all-to-all-start.1 = ((s32[128,1,64]{2,1,0:T(1,128)}), s32[128,1,64]{2,1,0:T(1,128)S(1)}, u32[]{:S(2)}, u32[]{:S(2)}) async-start(s32[128,1,64]{2,1,0:T(1,128)} %bitcast.2), calls=%async_computation.1 | async-start | bytes 131072 | tf_op jit(solution)/shard_map/all_to_all | solution.py:45
  20.0 0.7 iota_compare_fusion
  20.7 0.8 copy.29
  21.6 0.1 reshape.146
  21.7 4.5 %broadcast_select_fusion = bf16[128,64,128]{2,1,0:T(8,128)(2,1)} fusion(bf16[128,64,128]{2,1,0:T(8,128)(2,1)} %param.15, pred[128,64]{1,0:T(8,128)(4,1)S(1)} %iota_compare_fusion), kind=kLoop, calls=%fused_computation.10 | loop fusion | flops 1048576 | bytes 4202496 | tf_op jit(solution)/shard_map/jit(_where)/select_n | solution.py:42
  26.3 2.8 multiply_convert_fusion.1
  29.1 1.6 multiply_convert_fusion.3
  30.7 0.3 copy-done.2
  31.1 0.4 divide_select_fusion
  31.5 10.3 %all-to-all-start = ((bf16[128,64,128]{2,1,0:T(8,128)(2,1)}), bf16[128,64,128]{2,1,0:T(8,128)(2,1)}, u32[]{:S(2)}, u32[]{:S(2)}) async-start(bf16[128,64,128]{2,1,0:T(8,128)(2,1)} %broadcast_select_fusion), calls=%async_computation | async-start | bytes 4194304 | tf_op jit(solution)/shard_map/all_to_all | solution.py:44
  41.8 0.5 broadcast.153
  42.4 0.8 reduce.10
  43.2 0.1 reshape.148
  43.3 27.8 %gather_fusion = f32[8192,128]{1,0:T(8,128)} fusion(f32[1024,128]{1,0:T(8,128)S(1)} %divide_select_fusion, s32[8192]{0:T(1024)S(1)} %broadcast_clamp_fusion.1), kind=kCustom, calls=%fused_computation | custom fusion | bytes 8421376 | tf_op jit(solution)/shard_map/jit(_take)/gather | solution.py:50
  71.1 0.7 all-to-all-done
  71.8 5.5 %multiply_reduce_fusion = f32[128,64]{1,0:T(8,128)} fusion(f32[128,64,128]{2,1,0:T(8,128)} %bitcast.30, pred[128,64]{1,0:T(8,128)(4,1)S(1)} %compare_and_fusion, bf16[128,64,128]{2,1,0:T(8,128)(2,1)} %all-to-all-done), kind=kLoop, calls=%fused_computation.5 | loop fusion | flops 4186112 | bytes 6332416 | tf_op jit(solution)/shard_map/reduce_sum | solution.py:51
  77.3 9.0 %all-to-all-start.2 = ((f32[128,1,64]{2,1,0:T(1,128)}), f32[128,1,64]{2,1,0:T(1,128)S(1)}, u32[]{:S(2)}, u32[]{:S(2)}) async-start(f32[128,1,64]{2,1,0:T(1,128)} %bitcast.6), calls=%async_computation.2 | async-start | bytes 131072 | tf_op jit(solution)/shard_map/all_to_all | solution.py:52
  86.3 0.0 all-reduce.9.cloned.1.call-start
  86.4 0.2 fusion.3
  86.6 8.9 %all-to-all-done.2 = f32[128,1,64]{2,1,0:T(1,128)S(1)} async-done(((f32[128,1,64]{2,1,0:T(1,128)}), f32[128,1,64]{2,1,0:T(1,128)S(1)}, u32[]{:S(2)}, u32[]{:S(2)}) %all-to-all-start.2) | async-done | bytes 32800 | tf_op jit(solution)/shard_map/all_to_all | solution.py:52
  95.6 0.5 broadcast.154
  96.1 0.8 reduce.11
  96.9 0.1 reshape.171
  97.0 57.0 %scatter_fusion = f32[1024]{0:T(1024)S(1)} fusion(f32[1024]{0:T(1024)S(1)} %bitcast.29, s32[8192]{0:T(1024)S(1)} %bitcast.32, f32[8192]{0:T(1024)S(1)} %reshape.171), kind=kCustom, calls=%fused_computation.2 | custom fusion | flops 8192 | bytes 131072 | tf_op jit(solution)/shard_map/scatter-add | solution.py:54
  154.0 0.6 fusion.2
  154.6 1.8 convert_reduce_fusion.1
  156.4 2.5 fusion.4
  158.9 1.0 convert_reduce_fusion
  159.9 2.6 convolution_bitcast_fusion
  162.5 0.0 all-reduce.9.cloned.1.call-update
  162.5 0.0 all-reduce.7.cloned.1.call-start
  162.6 32.9 %gather_fusion.1 = f32[8192]{0:T(1024)S(1)} fusion(f32[1024]{0:T(1024)S(1)} %get-tuple-element.46, s32[8192]{0:T(1024)S(1)} %broadcast_clamp_fusion), kind=kCustom, calls=%fused_computation.1 | custom fusion | bytes 98304 | tf_op jit(solution)/shard_map/jit(_take)/gather | solution.py:62
  195.5 0.1 gather.15
  195.6 30.7 %all-reduce.9.cloned.1.call-done = (f32[1024,512]{0,1:T(8,128)}, f32[512,256]{1,0:T(8,128)}) async-done(((f32[1024,512]{0,1:T(8,128)}, f32[512,256]{1,0:T(8,128)}), (f32[1024,512]{0,1:T(8,128)}, f32[512,256]{1,0:T(8,128)})) %all-reduce.9.cloned.1.call-update) | async-done | bytes 2621456 | tf_op jit(solution)/shard_map/psum | solution.py:91
  226.3 0.0 all-reduce.7.cloned.1.call-update
  226.3 0.6 and_select_fusion
  226.9 8.4 %all-to-all-start.3 = ((f32[128,1,64]{2,1,0:T(1,128)}), f32[128,1,64]{2,1,0:T(1,128)S(1)}, u32[]{:S(2)}, u32[]{:S(2)}) async-start(f32[128,1,64]{2,1,0:T(1,128)} %bitcast.9), calls=%async_computation.3 | async-start | bytes 131072 | tf_op jit(solution)/shard_map/all_to_all | solution.py:63
  235.4 0.2 fusion.5
  235.5 15.0 %all-reduce.2 = (f32[512]{0:T(512)S(1)}, f32[256]{0:T(256)S(1)}, f32[256]{0:T(256)S(1)}) all-reduce(f32[512]{0:T(512)S(1)} %get-tuple-element.54, f32[256]{0:T(256)S(1)} %get-tuple-element.42, f32[256]{0:T(256)S(1)} %bitcast.36), channel_id=1, replica_groups=mesh['blk'=16,'rep'=8] {'rep'}, use_global_device_ids=true, to_apply=%region_6.7 | all-reduce | flops 1024 | bytes 8192 | tf_op jit(solution)/shard_map/psum | solution.py:91
  250.5 42.1 %all-reduce = (f32[512]{0:T(512)}, f32[256]{0:T(256)}, f32[256]{0:T(256)}) all-reduce(f32[512]{0:T(512)S(1)} %get-tuple-element.37, f32[256]{0:T(256)S(1)} %get-tuple-element.38, f32[256]{0:T(256)S(1)} %get-tuple-element.39), channel_id=1, replica_groups=mesh['blk'=16,'rep'=8] {'blk'}, use_global_device_ids=true, to_apply=%region_7.8 | all-reduce | flops 1024 | bytes 8192 | tf_op jit(solution)/shard_map/psum | solution.py:90
  292.6 0.8 reduce.12
  293.4 0.1 mul.66
  293.5 3.8 %bitcast_multiply_fusion = f32[8192,128]{1,0:T(8,128)} fusion(f32[8192]{0:T(1024)S(1)} %mul.66, bf16[128,64,128]{2,1,0:T(8,128)(2,1)} %all-to-all-done), kind=kLoop, calls=%fused_computation.4 | loop fusion | flops 2097152 | bytes 6324224 | tf_op jit(solution)/shard_map/mul | solution.py:66
  297.3 45.1 %scatter_custom_fusion.1 = f32[1024,128]{1,0:T(8,128)} fusion(s32[8192]{0:T(1024)S(1)} %bitcast.35, f32[8192,128]{1,0:T(8,128)} %bitcast_multiply_fusion, f32[]{:T(128)} %constant.32.clone.1), kind=kCustom, calls=%fused_computation.21 | custom fusion | flops 1048576 | bytes 524800 | tf_op jit(solution)/shard_map/scatter-add | solution.py:67
  342.4 2.7 multiply_subtract_fusion
  345.1 2.9 copy.35
  348.0 0.8 copy.41
  (40 shorter events, 0.2 us)
Async XLA Ops:
  7.2 19.1 %copy-start = (bf16[1024,1024]{1,0:T(8,128)(2,1)S(1)}, bf16[1024,1024]{1,0:T(8,128)(2,1)}, u32[]{:S(2)}) copy-start(bf16[1024,1024]{1,0:T(8,128)(2,1)} %param.13) | copy-start | bytes 6291460
  8.8 22.7 %all-to-all-start.1 = ((s32[128,1,64]{2,1,0:T(1,128)}), s32[128,1,64]{2,1,0:T(1,128)S(1)}, u32[]{:S(2)}, u32[]{:S(2)}) async-start(s32[128,1,64]{2,1,0:T(1,128)} %bitcast.2), calls=%async_computation.1 | async-start | bytes 131072 | tf_op jit(solution)/shard_map/all_to_all | solution.py:45
  21.7 4.6 %copy-start.7 = (bf16[1024,512]{1,0:T(8,128)(2,1)S(1)}, bf16[1024,512]{1,0:T(8,128)(2,1)}, u32[]{:S(2)}) copy-start(bf16[1024,512]{1,0:T(8,128)(2,1)} %param.21) | copy-start | bytes 3145732
  21.7 4.6 %copy-start.10 = (f32[512]{0:T(512)S(1)}, f32[512]{0:T(512)}, u32[]{:S(2)}) copy-start(f32[512]{0:T(512)} %param.22) | copy-start | bytes 6148
  26.3 2.8 copy-start.8
  26.3 2.8 copy-start.11
  29.1 1.6 copy-start.13
  29.1 1.6 copy-start.1
  29.1 2.0 copy-start.2
  29.1 2.4 copy-start.12
  31.5 40.3 %all-to-all-start = ((bf16[128,64,128]{2,1,0:T(8,128)(2,1)}), bf16[128,64,128]{2,1,0:T(8,128)(2,1)}, u32[]{:S(2)}, u32[]{:S(2)}) async-start(bf16[128,64,128]{2,1,0:T(8,128)(2,1)} %broadcast_select_fusion), calls=%async_computation | async-start | bytes 4194304 | tf_op jit(solution)/shard_map/all_to_all | solution.py:44
  71.8 14.6 %copy-start.4 = (bf16[1024,256]{1,0:T(8,128)(2,1)S(1)}, bf16[1024,256]{1,0:T(8,128)(2,1)}, u32[]{:S(2)}) copy-start(bf16[1024,256]{1,0:T(8,128)(2,1)} %get-tuple-element.52) | copy-start | bytes 1572868
  77.3 18.3 %all-to-all-start.2 = ((f32[128,1,64]{2,1,0:T(1,128)}), f32[128,1,64]{2,1,0:T(1,128)S(1)}, u32[]{:S(2)}, u32[]{:S(2)}) async-start(f32[128,1,64]{2,1,0:T(1,128)} %bitcast.6), calls=%async_computation.2 | async-start | bytes 131072 | tf_op jit(solution)/shard_map/all_to_all | solution.py:52
  86.3 139.9 %all-reduce.9.cloned.1.call-start = ((), (), s32[]{:S(2)}) async-start(), calls=%async_computation.5 | async-start | bytes 5242880 | tf_op jit(solution)/shard_map/psum | solution.py:91
  97.0 57.0 %copy-start.6 = (s32[1024]{0:T(1024)S(1)}, s32[1024]{0:T(1024)}, u32[]{:S(2)}) copy-start(s32[1024]{0:T(1024)} %param.14) | copy-start | bytes 12292
  154.0 4.9 %copy-start.9 = (bf16[512,256]{1,0:T(8,128)(2,1)S(1)}, bf16[512,256]{1,0:T(8,128)(2,1)}, u32[]{:S(2)}) copy-start(bf16[512,256]{1,0:T(8,128)(2,1)} %param.23) | copy-start | bytes 786436
  154.0 4.9 %copy-start.14 = (f32[1024,512]{1,0:T(8,128)S(1)}, f32[1024,512]{1,0:T(8,128)}, u32[]{:S(2)}) copy-start(f32[1024,512]{1,0:T(8,128)} %get-tuple-element.51) | copy-start | bytes 6291460
  162.5 182.5 %all-reduce.7.cloned.1.call-start = ((), (), s32[]{:S(2)}) async-start(), calls=%async_computation.4 | async-start | bytes 5242880 | tf_op jit(solution)/shard_map/psum | solution.py:90
  226.9 65.7 %all-to-all-start.3 = ((f32[128,1,64]{2,1,0:T(1,128)}), f32[128,1,64]{2,1,0:T(1,128)S(1)}, u32[]{:S(2)}, u32[]{:S(2)}) async-start(f32[128,1,64]{2,1,0:T(1,128)} %bitcast.9), calls=%async_computation.3 | async-start | bytes 131072 | tf_op jit(solution)/shard_map/all_to_all | solution.py:63
  293.5 48.9 %copy-start.3 = (f32[1024,128]{1,0:T(8,128)S(1)}, f32[1024,128]{1,0:T(8,128)}, u32[]{:S(2)}) copy-start(f32[1024,128]{1,0:T(8,128)} %param.20) | copy-start | bytes 1572868
  345.1 2.9 copy-start.5
Sparse Core Ops, SparseCore 0:
  162.6 63.5 all-reduce.8
  229.7 92.9 all-reduce.6
